TPU v7x, 256 devices: a whole 4x4x8 slice. The times are simulated.
256 devices in a mesh: expert: 32 (over y, x, core), dp: 8 (over z).
Axes of the slice: x: 4, y: 4, z: 8, core: 2. Of those that a mesh axis runs over, the one named last changes fastest.
Arguments:
- tokens: bfloat16 [32768, 2048], P(('expert', 'dp')), may hold values from -6 to 6
- cotangent: bfloat16 [32768, 2048], P(('expert', 'dp')), may hold values from -6 to 6
- routes: int32 [32768, 4], P(('expert', 'dp')), may hold values from 0 to 31, all different within a row; in each aligned block of 128 rows (0 to 127, 128 to 255, ...) at most 24 rows name the same one
- gate_values: bfloat16 [32768, 4], P(('expert', 'dp')), may hold values from 0.099609375 to 1
- w_gate: bfloat16 [32, 2048, 512], P('expert', 'dp'), may hold values from -0.125 to 0.125
- w_up: bfloat16 [32, 2048, 512], P('expert', 'dp'), may hold values from -0.125 to 0.125
- w_down: bfloat16 [32, 512, 2048], P('expert', None, 'dp'), may hold values from -0.25 to 0.25
Outputs:
- token_grad: bfloat16 [32768, 2048], P(('expert', 'dp'))
- gate_weight_grad: bfloat16 [32, 2048, 512], P('expert', 'dp')
- up_weight_grad: bfloat16 [32, 2048, 512], P('expert', 'dp')
- down_weight_grad: bfloat16 [32, 512, 2048], P('expert', None, 'dp')
Inputs may be any that keep to these rules, and one draw needn't show every extreme that they name: `routes`: each row names 4 different experts. Among the rows of one device no expert is named more than 24 times, and some device names some expert exactly 24 times.
All inputs are finite; a program needn't handle non-finite values.
Results may differ from a plain program's by a relative error of at most 0.017.
Values may be sent and summed in bfloat16 or wider, within the bound.
No kernel may reach another device: no remote copies, remote signals or barrier semaphores. Data moves between devices by JAX's collectives and lax.ppermute only.
A program may use at most 128 MiB of HBM per device.

v0:
```python
import jax
import jax.numpy as jnp
from jax import lax
from jax.sharding import PartitionSpec as P


def place_slots(routes, experts, capacity):
    expert_ids = routes.reshape(-1)
    onehot = (expert_ids[:, None] == jnp.arange(experts, dtype=jnp.int32)[None, :]).astype(
        jnp.int32
    )
    before = jnp.cumsum(onehot, axis=0) - onehot
    slot = jnp.sum(before * onehot, axis=1)
    return expert_ids * capacity + slot


def forward_part(x_rows, weight_gate, weight_up):
    gate_pre = jnp.dot(x_rows, weight_gate, preferred_element_type=jnp.float32)
    up_pre = jnp.dot(x_rows, weight_up, preferred_element_type=jnp.float32)
    sigmoid_gate = 1.0 / (1.0 + jnp.exp(-gate_pre))
    activated = gate_pre * sigmoid_gate
    hidden = (activated * up_pre).astype(jnp.bfloat16)
    return (gate_pre, up_pre, sigmoid_gate, activated, hidden)


def local(tokens, cotangent, routes, gate_values, w_gate, w_up, w_down):
    experts = lax.axis_size("expert")
    tok_dev, model_width = tokens.shape
    fan_out = routes.shape[1]
    capacity = min(tok_dev, 3 * tok_dev * fan_out // (2 * experts))
    slot_index = place_slots(routes, experts, capacity)
    source_tok = jnp.arange(tok_dev * fan_out, dtype=jnp.int32) // fan_out

    def pack_rows(values):
        buffer = (
            jnp.zeros((experts * capacity, model_width), values.dtype)
            .at[slot_index]
            .set(values[source_tok])
        )
        return buffer.reshape(experts, capacity, model_width)

    gate_slots = (
        jnp.zeros((experts * capacity,), gate_values.dtype)
        .at[slot_index]
        .set(gate_values.reshape(-1))
    )
    gate_slots = gate_slots.reshape(experts, capacity)
    full_gate, full_up, full_down = (
        lax.all_gather(w_gate, "dp", axis=1, tiled=True),
        lax.all_gather(w_up, "dp", axis=1, tiled=True),
        lax.all_gather(w_down, "dp", axis=2, tiled=True),
    )
    full_gate = full_gate[0]
    full_up = full_up[0]
    recv_x, recv_dy, recv_gate = (
        lax.all_to_all(pack_rows(tokens), "expert", split_axis=0, concat_axis=0, tiled=True),
        lax.all_to_all(pack_rows(cotangent), "expert", split_axis=0, concat_axis=0, tiled=True),
        lax.all_to_all(gate_slots, "expert", split_axis=0, concat_axis=0, tiled=True),
    )
    x_rows = recv_x.reshape(-1, model_width)
    gate_pre, up_pre, sigmoid_gate, activated, hidden = forward_part(x_rows, full_gate, full_up)
    dy_rows = recv_dy.reshape(-1, model_width)
    scaled = (recv_gate.reshape(-1, 1).astype(jnp.float32) * dy_rows.astype(jnp.float32)).astype(
        jnp.bfloat16
    )
    hidden_grad = lax.dot_general(
        scaled, full_down[0], (((1,), (1,)), ((), ())), preferred_element_type=jnp.float32
    )
    down_term = lax.dot_general(
        hidden, scaled, (((0,), (0,)), ((), ())), preferred_element_type=jnp.float32
    )
    gate_grad = (
        hidden_grad * up_pre * sigmoid_gate * (1.0 + gate_pre * (1.0 - sigmoid_gate))
    ).astype(jnp.bfloat16)
    up_grad = (hidden_grad * activated).astype(jnp.bfloat16)
    row_grad = lax.dot_general(
        gate_grad, full_gate, (((1,), (1,)), ((), ())), preferred_element_type=jnp.float32
    )
    row_grad = row_grad + lax.dot_general(
        up_grad, full_up, (((1,), (1,)), ((), ())), preferred_element_type=jnp.float32
    )
    returned = lax.all_to_all(
        row_grad.astype(jnp.bfloat16).reshape(experts, capacity, model_width),
        "expert",
        split_axis=0,
        concat_axis=0,
        tiled=True,
    )
    picked = returned.reshape(experts * capacity, model_width)[slot_index]
    token_grad = jnp.sum(
        picked.astype(jnp.float32).reshape(tok_dev, fan_out, model_width), axis=1
    ).astype(jnp.bfloat16)
    gate_term = lax.dot_general(
        x_rows, gate_grad, (((0,), (0,)), ((), ())), preferred_element_type=jnp.float32
    )
    up_term = lax.dot_general(
        x_rows, up_grad, (((0,), (0,)), ((), ())), preferred_element_type=jnp.float32
    )
    gate_sum, up_sum, down_sum = (
        lax.psum_scatter(
            gate_term[None].astype(jnp.bfloat16), "dp", scatter_dimension=1, tiled=True
        ).astype(jnp.float32),
        lax.psum_scatter(
            up_term[None].astype(jnp.bfloat16), "dp", scatter_dimension=1, tiled=True
        ).astype(jnp.float32),
        lax.psum_scatter(
            down_term[None].astype(jnp.bfloat16), "dp", scatter_dimension=2, tiled=True
        ).astype(jnp.float32),
    )
    return (
        token_grad,
        gate_sum.astype(jnp.bfloat16),
        up_sum.astype(jnp.bfloat16),
        down_sum.astype(jnp.bfloat16),
    )


def solution(mesh):
    in_specs = (
        P(("expert", "dp"), None),
        P(("expert", "dp"), None),
        P(("expert", "dp"), None),
        P(("expert", "dp"), None),
        P("expert", "dp", None),
        P("expert", "dp", None),
        P("expert", None, "dp"),
    )
    out_specs = (
        P(("expert", "dp"), None),
        P("expert", "dp", None),
        P("expert", "dp", None),
        P("expert", None, "dp"),
    )
    return jax.shard_map(local, mesh=mesh, in_specs=in_specs, out_specs=out_specs, check_vma=False)
```

profile of v0, /device:TPU:2, one launch (start us, length us, event | category | flops | bytes accessed | tf_op | source)
XLA Modules:
  0.0 282.5 jit_solution(12126324766856364490)
XLA Ops:
  12.3 3.8 %scatter_custom_fusion = bf16[768]{0:T(1024)(128)(2,1)S(1)} fusion(s32[512]{0:T(512)S(1)} %bitcast.72, bf16[512]{0:T(512)(128)(2,1)S(1)} %reshape.185, bf16[]{:T(256)} %constant.27.clone.1), kind=kCustom, calls=%fused_computation.54 | custom fusion | bytes 1538 | tf_op jit(solution)/shard_map/scatter | solution.py:45
  16.8 7.9 %all-to-all-start = ((bf16[32,1,24]{2,1,0:T(2,128)(2,1)}), bf16[32,1,24]{2,1,0:T(2,128)(2,1)S(1)}, u32[]{:S(2)}, u32[]{:S(2)}) async-start(bf16[32,1,24]{2,1,0:T(2,128)(2,1)} %all_to_all.20), calls=%async_computation | async-start | bytes 32768 | tf_op jit(solution)/shard_map/all_to_all | solution.py:58
  24.8 12.3 %scatter_custom_fusion.1 = bf16[768,2048]{1,0:T(8,128)(2,1)} fusion(s32[512]{0:T(512)S(1)} %bitcast.73, bf16[128,2048]{1,0:T(8,128)(2,1)S(1)} %copy-done, s32[1024]{0:T(1024)S(1)} %pad_clamp_fusion.1, bf16[]{:T(256)} %constant.27.clone.1), kind=kCustom, calls=%fused_computation.27 | custom fusion | bytes 3145730 | tf_op jit(solution)/shard_map/scatter | solution.py:38
  37.1 7.4 %all-to-all-start.1 = ((bf16[32,24,2048]{2,1,0:T(8,128)(2,1)}), bf16[32,24,2048]{2,1,0:T(8,128)(2,1)}, u32[]{:S(2)}, u32[]{:S(2)}) async-start(bf16[32,24,2048]{2,1,0:T(8,128)(2,1)} %bitcast.68), calls=%async_computation.1 | async-start | bytes 6291456 | tf_op jit(solution)/shard_map/all_to_all | solution.py:57
  45.3 11.9 %scatter_custom_fusion.2 = bf16[768,2048]{1,0:T(8,128)(2,1)} fusion(s32[512]{0:T(512)S(1)} %bitcast.74, bf16[128,2048]{1,0:T(8,128)(2,1)} %param.7, s32[1024]{0:T(1024)S(1)} %pad_clamp_fusion.1, bf16[]{:T(256)} %constant.27.clone.1), kind=kCustom, calls=%fused_computation.25 | custom fusion | bytes 3146240 | tf_op jit(solution)/shard_map/scatter | solution.py:38
  57.1 27.1 %all-to-all-done.1 = bf16[32,24,2048]{2,1,0:T(8,128)(2,1)} async-done(((bf16[32,24,2048]{2,1,0:T(8,128)(2,1)}), bf16[32,24,2048]{2,1,0:T(8,128)(2,1)}, u32[]{:S(2)}, u32[]{:S(2)}) %all-to-all-start.1) | async-done | bytes 3145760 | tf_op jit(solution)/shard_map/all_to_all | solution.py:57
  84.2 6.8 %all-to-all-start.2 = ((bf16[32,24,2048]{2,1,0:T(8,128)(2,1)}), bf16[32,24,2048]{2,1,0:T(8,128)(2,1)}, u32[]{:S(2)}, u32[]{:S(2)}) async-start(bf16[32,24,2048]{2,1,0:T(8,128)(2,1)} %bitcast.67), calls=%async_computation.2 | async-start | bytes 6291456 | tf_op jit(solution)/shard_map/all_to_all | solution.py:56
  92.3 4.1 %fusion = bf16[768,2048]{1,0:T(8,128)(2,1)} fusion(f32[768]{0:T(1024)S(1)} %reshape.155, bf16[32,24,2048]{2,1,0:T(8,128)(2,1)} %all-to-all-done.1), kind=kLoop, calls=%fused_computation.7 | loop fusion | flops 4718592 | bytes 6294528 | tf_op jit(solution)/shard_map/convert_element_type | solution.py:63
  96.4 34.4 %all-to-all-done.2 = bf16[32,24,2048]{2,1,0:T(8,128)(2,1)} async-done(((bf16[32,24,2048]{2,1,0:T(8,128)(2,1)}), bf16[32,24,2048]{2,1,0:T(8,128)(2,1)}, u32[]{:S(2)}, u32[]{:S(2)}) %all-to-all-start.2) | async-done | bytes 3145760 | tf_op jit(solution)/shard_map/all_to_all | solution.py:56
  130.8 4.3 %fusion.6 = f32[768,512]{1,0:T(8,128)S(1)} fusion(bf16[768,2048]{1,0:T(8,128)(2,1)} %bitcast.9, bf16[1,2048,512]{2,1,0:T(8,128)(2,1)} %all-gather.8.cloned.1.call-done), kind=kOutput, calls=%fused_computation.18 | convolution fusion | flops 1610612736 | bytes 6815744 | tf_op jit(solution)/shard_map/dot_general | solution.py:18
  135.2 4.5 %fusion.9 = f32[768,512]{1,0:T(8,128)S(1)} fusion(bf16[768,2048]{1,0:T(8,128)(2,1)} %bitcast.9, bf16[1,2048,512]{2,1,0:T(8,128)(2,1)} %all-gather.6.cloned.1.call-done), kind=kOutput, calls=%fused_computation.21 | convolution fusion | flops 1610612736 | bytes 6815744 | tf_op jit(solution)/shard_map/dot_general | solution.py:19
  140.8 3.3 %fusion.3 = bf16[1,512,2048]{2,1,0:T(8,128)(2,1)} fusion(bf16[768,2048]{1,0:T(8,128)(2,1)S(1)} %copy-done.1, f32[768,512]{1,0:T(8,128)S(1)} %fusion.9, f32[768,512]{1,0:T(8,128)S(1)} %fusion.6), kind=kOutput, calls=%fused_computation.15 | convolution fusion | flops 1614020608 | bytes 8388608 | tf_op jit(solution)/shard_map/dot_general | solution.py:69
  144.3 4.2 %multiply_convert_fusion = bf16[32,24,2048]{2,1,0:T(8,128)(2,1)} fusion(f32[32,24]{1,0:T(8,128)S(1)} %bitcast.71, bf16[32,24,2048]{2,1,0:T(8,128)(2,1)} %all-to-all-done.1), kind=kLoop, calls=%fused_computation.9 | loop fusion | flops 4718592 | bytes 6294528 | tf_op jit(solution)/shard_map/convert_element_type | solution.py:63
  148.4 5.2 %multiply_convert_fusion.2 = (bf16[768,512]{1,0:T(8,128)(2,1)S(1)}, bf16[768,512]{1,0:T(8,128)(2,1)S(1)}) fusion(f32[768,512]{1,0:T(8,128)S(1)} %fusion.6, f32[768,512]{1,0:T(8,128)} %copy-done.5, bf16[768,2048]{1,0:T(8,128)(2,1)} %bitcast.70, bf16[1,512,2048]{2,1,0:T(8,128)(2,1)} %all-gather.4.cloned.1.call-done), kind=kOutput, calls=%fused_computation.30 | convolution fusion | flops 1615724544 | bytes 9961472 | tf_op jit(solution)/shard_map/dot_general | solution.py:66
  154.6 5.1 %fusion.1 = bf16[1,2048,512]{2,1,0:T(8,128)(2,1)} fusion(bf16[768,2048]{1,0:T(8,128)(2,1)} %bitcast.9, bf16[768,512]{1,0:T(8,128)(2,1)S(1)} %get-tuple-element.5), kind=kOutput, calls=%fused_computation.13 | convolution fusion | flops 1611661312 | bytes 6029312 | tf_op jit(solution)/shard_map/dot_general | solution.py:93
  159.9 5.1 %fusion.2 = bf16[1,2048,512]{2,1,0:T(8,128)(2,1)} fusion(bf16[768,2048]{1,0:T(8,128)(2,1)} %bitcast.9, bf16[768,512]{1,0:T(8,128)(2,1)S(1)} %get-tuple-element.4), kind=kOutput, calls=%fused_computation.14 | convolution fusion | flops 1611661312 | bytes 6029312 | tf_op jit(solution)/shard_map/dot_general | solution.py:96
  166.6 3.1 %fusion.4 = f32[768,2048]{1,0:T(8,128)S(1)} fusion(bf16[768,512]{1,0:T(8,128)(2,1)} %copy-done.4, bf16[1,2048,512]{2,1,0:T(8,128)(2,1)S(1)} %copy-done.2), kind=kOutput, calls=%fused_computation.16 | convolution fusion | flops 1610612736 | bytes 9175040 | tf_op jit(solution)/shard_map/dot_general | solution.py:76
  169.7 3.5 %add_convert_fusion = bf16[768,2048]{1,0:T(8,128)(2,1)} fusion(f32[768,2048]{1,0:T(8,128)S(1)} %fusion.4, bf16[768,512]{1,0:T(8,128)(2,1)S(1)} %get-tuple-element.4, bf16[1,2048,512]{2,1,0:T(8,128)(2,1)S(1)} %copy-done.3), kind=kOutput, calls=%fused_computation.8 | convolution fusion | flops 1613758464 | bytes 12320768 | tf_op jit(solution)/shard_map/dot_general | solution.py:79
  173.3 7.0 %all-to-all-start.3 = ((bf16[32,24,2048]{2,1,0:T(8,128)(2,1)}), bf16[32,24,2048]{2,1,0:T(8,128)(2,1)}, u32[]{:S(2)}, u32[]{:S(2)}) async-start(bf16[32,24,2048]{2,1,0:T(8,128)(2,1)} %bitcast.69), calls=%async_computation.3 | async-start | bytes 6291456 | tf_op jit(solution)/shard_map/all_to_all | solution.py:82
  180.3 39.8 %all-to-all-done.3 = bf16[32,24,2048]{2,1,0:T(8,128)(2,1)} async-done(((bf16[32,24,2048]{2,1,0:T(8,128)(2,1)}), bf16[32,24,2048]{2,1,0:T(8,128)(2,1)}, u32[]{:S(2)}, u32[]{:S(2)}) %all-to-all-start.3) | async-done | bytes 3145760 | tf_op jit(solution)/shard_map/all_to_all | solution.py:82
  220.1 6.7 %gather_fusion = bf16[512,2048]{1,0:T(8,128)(2,1)S(1)} fusion(bf16[768,2048]{1,0:T(8,128)(2,1)} %bitcast.13, s32[1024]{0:T(1024)S(1)} %pad_clamp_fusion), kind=kCustom, calls=%fused_computation.2 | custom fusion | bytes 4196352 | tf_op jit(solution)/shard_map/gather | solution.py:89
  226.8 2.3 gather.14
  229.1 5.0 %reduce_sum.25 = bf16[128,2048]{1,0:T(8,128)(2,1)} reduce(bf16[128,4,2048]{2,1,0:T(4,128)(2,1)} %gather.14, bf16[]{:T(256)} %constant.27.clone.1), dimensions={1}, to_apply=%region_6.7 | reduce | flops 786432 | bytes 2621442 | tf_op jit(solution)/shard_map/reduce_sum | solution.py:90
  234.1 41.3 %reduce-scatter.6.cloned.1.call-done = bf16[1,256,512]{2,1,0:T(8,128)(2,1)} async-done(((bf16[1,2048,512]{2,1,0:T(8,128)(2,1)}), bf16[1,256,512]{2,1,0:T(8,128)(2,1)}) %reduce-scatter.6.cloned.1.call-update) | async-done | bytes 262160 | tf_op jit(solution)/shard_map/reduce_scatter | solution.py:103
  (52 shorter events, 11.9 us)
Async XLA Ops:
  7.2 17.6 %copy-start = (bf16[128,2048]{1,0:T(8,128)(2,1)S(1)}, bf16[128,2048]{1,0:T(8,128)(2,1)}, u32[]{:S(2)}) copy-start(bf16[128,2048]{1,0:T(8,128)(2,1)} %param.8) | copy-start | bytes 1572868
  7.2 123.6 %all-gather.8.cloned.1.call-start = ((), (), s32[]{:S(2)}) async-start(), calls=%async_computation.9 | async-start | bytes 2359296 | tf_op jit(solution)/shard_map/all_gather | solution.py:49
  16.8 20.3 %all-to-all-start = ((bf16[32,1,24]{2,1,0:T(2,128)(2,1)}), bf16[32,1,24]{2,1,0:T(2,128)(2,1)S(1)}, u32[]{:S(2)}, u32[]{:S(2)}) async-start(bf16[32,1,24]{2,1,0:T(2,128)(2,1)} %all_to_all.20), calls=%async_computation | async-start | bytes 32768 | tf_op jit(solution)/shard_map/all_to_all | solution.py:58
  37.1 47.2 %all-to-all-start.1 = ((bf16[32,24,2048]{2,1,0:T(8,128)(2,1)}), bf16[32,24,2048]{2,1,0:T(8,128)(2,1)}, u32[]{:S(2)}, u32[]{:S(2)}) async-start(bf16[32,24,2048]{2,1,0:T(8,128)(2,1)} %bitcast.68), calls=%async_computation.1 | async-start | bytes 6291456 | tf_op jit(solution)/shard_map/all_to_all | solution.py:57
  44.5 90.7 %all-gather.6.cloned.1.call-start = ((), (), s32[]{:S(2)}) async-start(), calls=%async_computation.8 | async-start | bytes 2359296 | tf_op jit(solution)/shard_map/all_gather | solution.py:50
  84.2 46.6 %all-to-all-start.2 = ((bf16[32,24,2048]{2,1,0:T(8,128)(2,1)}), bf16[32,24,2048]{2,1,0:T(8,128)(2,1)}, u32[]{:S(2)}, u32[]{:S(2)}) async-start(bf16[32,24,2048]{2,1,0:T(8,128)(2,1)} %bitcast.67), calls=%async_computation.2 | async-start | bytes 6291456 | tf_op jit(solution)/shard_map/all_to_all | solution.py:56
  91.0 57.4 %all-gather.4.cloned.1.call-start = ((), (), s32[]{:S(2)}) async-start(), calls=%async_computation.7 | async-start | bytes 2359296 | tf_op jit(solution)/shard_map/all_gather | solution.py:51
  91.7 142.4 %reduce-scatter.8.cloned.1.call-start = ((), (), s32[]{:S(2)}) async-start(), calls=%async_computation.12 | async-start | bytes 2359296 | tf_op jit(solution)/shard_map/reduce_scatter | solution.py:106
  135.2 5.6 %copy-start.1 = (bf16[768,2048]{1,0:T(8,128)(2,1)S(1)}, bf16[768,2048]{1,0:T(8,128)(2,1)}, u32[]{:S(2)}) copy-start(bf16[768,2048]{1,0:T(8,128)(2,1)} %fusion) | copy-start | bytes 9437188
  139.7 1.2 copy-start.5
  144.2 89.9 %reduce-scatter.4.cloned.1.call-start = ((), (), s32[]{:S(2)}) async-start(), calls=%async_computation.10 | async-start | bytes 2359296 | tf_op jit(solution)/shard_map/reduce_scatter | solution.py:100
  153.7 0.9 copy-start.4
  159.7 115.7 %reduce-scatter.6.cloned.1.call-start = ((), (), s32[]{:S(2)}) async-start(), calls=%async_computation.11 | async-start | bytes 2359296 | tf_op jit(solution)/shard_map/reduce_scatter | solution.py:103
  165.0 1.6 copy-start.2
  166.6 3.1 %copy-start.3 = (bf16[1,2048,512]{2,1,0:T(8,128)(2,1)S(1)}, bf16[1,2048,512]{2,1,0:T(8,128)(2,1)}, u32[]{:S(2)}) copy-start(bf16[1,2048,512]{2,1,0:T(8,128)(2,1)} %all-gather.6.cloned.1.call-done) | copy-start | bytes 6291460
  173.3 46.9 %all-to-all-start.3 = ((bf16[32,24,2048]{2,1,0:T(8,128)(2,1)}), bf16[32,24,2048]{2,1,0:T(8,128)(2,1)}, u32[]{:S(2)}, u32[]{:S(2)}) async-start(bf16[32,24,2048]{2,1,0:T(8,128)(2,1)} %bitcast.69), calls=%async_computation.3 | async-start | bytes 6291456 | tf_op jit(solution)/shard_map/all_to_all | solution.py:82
Sparse Core Ops, SparseCore 0:
  9.8 44.2 all-gather.7
  55.9 39.6 all-gather.5
  97.3 45.9 all-gather.3
  146.3 41.2 reduce-scatter.7
  190.5 41.0 reduce-scatter.3
  234.6 40.8 reduce-scatter.5
where the time goes:
time: 287 us; the launch traced here: 282 us
  waiting for transfers between devices  145 us (51%)
  local copies, waits for them, and re-layouts  43.7 us (15%)
  matrix products  34.2 us (12%)
  starting transfers between devices  30.2 us (11%)
  other arithmetic  15.4 us (5%)
  between operations  14.5 us (5%)
    reduce_scatter x1, waiting for transfers between devices, local(): lax.psum_scatter(up_term[None].astype(jnp.bfloat16), 'dp', scatter_dimens...  41.3 us
    all_to_all x1, waiting for transfers between devices, local(): lax.all_to_all(row_grad.astype(jnp.bfloat16).reshape(experts, capacity, m...  39.8 us
    all_to_all x1, waiting for transfers between devices, local(): lax.all_to_all(pack_rows(tokens), 'expert', split_axis=0, concat_axis=0,...  34.4 us
    all_to_all x1, waiting for transfers between devices, local(): lax.all_to_all(pack_rows(cotangent), 'expert', split_axis=0, concat_axis=...  27.1 us
    scatter x2, local copies, waits for them, and re-layouts, pack_rows(): buffer = jnp.zeros((experts * capacity, model_width), values.dtype).at[sl...  24.2 us
    gather x2, local copies, waits for them, and re-layouts, local(): picked = returned.reshape(experts * capacity, model_width)[slot_index]  8.96 us
    convert_element_type x2, other arithmetic, local(): (recv_gate.reshape(-1, 1).astype(jnp.float32) * dy_rows.astype(jnp.float3...  8.27 us
    all_to_all x1, starting transfers between devices, local(): lax.all_to_all(gate_slots, 'expert', split_axis=0, concat_axis=0, tiled=T...  7.9 us
  transfers between devices with their start and end apart: 10, of which 4 were waited for; matrix products, arithmetic and copies ran while one was open for 31% of the time, Pallas kernels for 0%

commit v1 on v0

v1 whole, which is shorter than its diff:
```python
import jax
import jax.numpy as jnp
from jax import lax
from jax.experimental.layout import Layout, with_layout_constraint
from jax.sharding import PartitionSpec as P


def slot_masks(routes, gate_values, experts, capacity):
    tok_dev = routes.shape[0]
    ids = jnp.arange(experts, dtype=jnp.int32)
    hit = routes[:, :, None] == ids[None, None, :]
    member = jnp.any(hit, axis=1)
    gate = jnp.sum(
        jnp.where(hit, gate_values.astype(jnp.float32)[:, :, None], 0.0), axis=1
    )
    row = lax.broadcasted_iota(jnp.int32, (tok_dev, tok_dev), 0)
    col = lax.broadcasted_iota(jnp.int32, (tok_dev, tok_dev), 1)
    earlier = (row < col).astype(jnp.bfloat16)
    before = lax.dot_general(
        member.astype(jnp.bfloat16),
        earlier,
        (((0,), (0,)), ((), ())),
        preferred_element_type=jnp.float32,
    ).astype(jnp.int32)
    rank = jnp.where(member.T, before, -1)
    place = rank[:, None, :] == jnp.arange(capacity, dtype=jnp.int32)[None, :, None]
    place = place.reshape(experts * capacity, tok_dev)
    weight = jnp.broadcast_to(gate.T[:, None, :], (experts, capacity, tok_dev)).reshape(
        experts * capacity, tok_dev
    )
    return place.astype(jnp.bfloat16), jnp.where(place, weight, 0.0).astype(jnp.bfloat16)


def row_major(a):
    return with_layout_constraint(a, Layout(major_to_minor=(0, 1)))


def matmul(a, b, dims):
    return lax.dot_general(a, b, (dims, ((), ())), preferred_element_type=jnp.float32)


def local(tokens, cotangent, routes, gate_values, w_gate, w_up, w_down):
    experts = lax.axis_size("expert")
    tok_dev, model_width = tokens.shape
    fan_out = routes.shape[1]
    hidden_width = w_gate.shape[2]
    capacity = min(tok_dev, 3 * tok_dev * fan_out // (2 * experts))

    shard = jnp.concatenate([w_gate[0], w_up[0], w_down[0].T], axis=1)
    full = row_major(lax.all_gather(row_major(shard), "dp", axis=0, tiled=True))

    place, weighted = slot_masks(routes, gate_values, experts, capacity)

    def exchange(rows):
        return lax.all_to_all(
            rows.reshape(experts, capacity, model_width),
            "expert",
            split_axis=0,
            concat_axis=0,
            tiled=True,
        ).reshape(experts * capacity, model_width)

    x_rows = exchange(matmul(place, tokens, ((1,), (0,))).astype(jnp.bfloat16))
    scaled = exchange(matmul(weighted, cotangent, ((1,), (0,))).astype(jnp.bfloat16))

    pre = matmul(x_rows, full[:, : 2 * hidden_width], ((1,), (0,)))
    gate_pre = pre[:, :hidden_width]
    up_pre = pre[:, hidden_width:]
    sigmoid_gate = 1.0 / (1.0 + jnp.exp(-gate_pre))
    activated = gate_pre * sigmoid_gate
    hidden = (activated * up_pre).astype(jnp.bfloat16)
    hidden_grad = matmul(scaled, full[:, 2 * hidden_width :], ((1,), (0,)))
    gate_grad = (
        hidden_grad * up_pre * sigmoid_gate * (1.0 + gate_pre * (1.0 - sigmoid_gate))
    ).astype(jnp.bfloat16)
    up_grad = (hidden_grad * activated).astype(jnp.bfloat16)
    both_grad = jnp.concatenate([gate_grad, up_grad], axis=1)

    in_term = matmul(x_rows, both_grad, ((0,), (0,))).astype(jnp.bfloat16)
    down_term = matmul(scaled, hidden, ((0,), (0,))).astype(jnp.bfloat16)
    terms = jnp.concatenate([in_term, down_term], axis=1)
    sums = row_major(lax.psum_scatter(row_major(terms), "dp", scatter_dimension=0, tiled=True))

    row_grad = matmul(both_grad, full[:, : 2 * hidden_width], ((1,), (1,)))
    returned = exchange(row_grad.astype(jnp.bfloat16))
    token_grad = matmul(place, returned, ((0,), (0,))).astype(jnp.bfloat16)
    return (
        token_grad,
        sums[None, :, :hidden_width],
        sums[None, :, hidden_width : 2 * hidden_width],
        sums[:, 2 * hidden_width :].T[None],
    )


def solution(mesh):
    in_specs = (
        P(("expert", "dp"), None),
        P(("expert", "dp"), None),
        P(("expert", "dp"), None),
        P(("expert", "dp"), None),
        P("expert", "dp", None),
        P("expert", "dp", None),
        P("expert", None, "dp"),
    )
    out_specs = (
        P(("expert", "dp"), None),
        P("expert", "dp", None),
        P("expert", "dp", None),
        P("expert", None, "dp"),
    )
    return jax.shard_map(local, mesh=mesh, in_specs=in_specs, out_specs=out_specs, check_vma=False)
```

time: 287 us -> 214 us (0.75); the launches traced: 282 us -> 213 us
  waiting for transfers between devices: 145 us -> 92.6 us
  blocking collectives: 0 us -> 43.7 us
  local copies, waits for them, and re-layouts: 43.7 us -> 4.04 us
  starting transfers between devices: 30.2 us -> 14.6 us
  other arithmetic: 15.4 us -> 6.23 us
  matrix products: 34.2 us -> 37.6 us
    all_to_all x4 -> x2, waiting for transfers between devices: 101 us -> 48.8 us  [exchange(): lax.all_to_all(rows.reshape(experts, capacity, model_width), 'expert', sp...]
    all_to_all x0 -> x1, blocking collectives: none -> 43.7 us  [exchange(): lax.all_to_all(rows.reshape(experts, capacity, model_width), 'expert', sp...]
    scatter x3 -> x0, local copies, waits for them, and re-layouts: 27.9 us -> none  [the longest x2 24.2 us: pack_rows(): buffer = jnp.zeros((experts * capacity, model_width), values.dtype).at[sl...]
    all_gather x3 -> x1, waiting for transfers between devices: 0.02 us -> 19.6 us  [local(): full = row_major(lax.all_gather(row_major(shard), 'dp', axis=0, tiled=True))]
    reduce_scatter x3 -> x1, waiting for transfers between devices: 41.3 us -> 24.2 us  [local(): lax.psum_scatter(row_major(terms), 'dp', scatter_dimension=0, tiled=True)]
    all_to_all x4 -> x2, starting transfers between devices: 29.1 us -> 14.6 us  [exchange(): lax.all_to_all(rows.reshape(experts, capacity, model_width), 'expert', sp...]
    gather x2 -> x0, local copies, waits for them, and re-layouts: 8.96 us -> none  [local(): picked = returned.reshape(experts * capacity, model_width)[slot_index]]
    convert_element_type x5 -> x2, other arithmetic: 8.35 us -> 0.17 us  [the longest x1 0.17 us: slot_masks(): jnp.where(place, weight, 0.0).astype(jnp.bfloat16)]
  transfers between devices with their start and end apart: 10 -> 4, of which waited for: 4 -> 4; matrix products, arithmetic and copies ran while one was open for 31% -> 10% of each run, Pallas kernels for 0% -> 0%
where the time goes in v1:
time: 214 us; the launch traced here: 213 us
  waiting for transfers between devices  92.6 us (43%)
  blocking collectives  43.7 us (20%)
  matrix products  37.6 us (18%)
  starting transfers between devices  14.6 us (7%)
  between operations  14.2 us (7%)
  other arithmetic  6.23 us (3%)
  local copies, waits for them, and re-layouts  4.04 us (2%)
    all_to_all x2, waiting for transfers between devices, exchange(): lax.all_to_all(rows.reshape(experts, capacity, model_width), 'expert', sp...  48.8 us
    all_to_all x1, blocking collectives, exchange(): lax.all_to_all(rows.reshape(experts, capacity, model_width), 'expert', sp...  43.7 us
    dot_general x8, matrix products, matmul(): lax.dot_general(a, b, (dims, ((), ())), preferred_element_type=jnp.float32)  37.5 us
    reduce_scatter x1, waiting for transfers between devices, local(): lax.psum_scatter(row_major(terms), 'dp', scatter_dimension=0, tiled=True)  24.2 us
    all_gather x1, waiting for transfers between devices, local(): full = row_major(lax.all_gather(row_major(shard), 'dp', axis=0, tiled=True))  19.6 us
    all_to_all x2, starting transfers between devices, exchange(): lax.all_to_all(rows.reshape(experts, capacity, model_width), 'expert', sp...  14.6 us
  transfers between devices with their start and end apart: 4, of which 4 were waited for; matrix products, arithmetic and copies ran while one was open for 10% of the time, Pallas kernels for 0%

profile of v1, /device:TPU:2, one launch (start us, length us, event | category | flops | bytes accessed | tf_op | source)
XLA Modules:
  0.0 213.1 jit_solution(319687289944547735)
XLA Ops:
  7.2 1.1 copy.38
  8.4 2.0 pad_maximum_fusion.4
  10.5 0.7 fusion.15
  11.2 0.1 fusion.11
  11.3 0.2 bitcast_compare_fusion
  11.5 2.6 %convolution_convert_fusion.1 = bf16[768,2048]{1,0:T(8,128)(2,1)} fusion(pred[768,128]{1,0:T(32,128)(4,1)S(1)} %bitcast_compare_fusion, bf16[128,2048]{1,0:T(8,128)(2,1)S(1)} %copy-done), kind=kOutput, calls=%fused_computation.7 | convolution fusion | flops 404226048 | bytes 3768320 | tf_op jit(solution)/shard_map/dot_general | solution.py:39
  14.1 7.8 %all-to-all-start.1 = ((bf16[32,24,2048]{2,1,0:T(8,128)(2,1)}), bf16[32,24,2048]{2,1,0:T(8,128)(2,1)}, u32[]{:S(2)}, u32[]{:S(2)}) async-start(bf16[32,24,2048]{2,1,0:T(8,128)(2,1)} %bitcast.43), calls=%async_computation.1 | async-start | bytes 6291456 | tf_op jit(solution)/shard_map/all_to_all | solution.py:55
  22.0 0.2 fusion.12
  22.2 2.6 %convolution_convert_fusion.2 = bf16[768,2048]{1,0:T(8,128)(2,1)} fusion(bf16[768,128]{1,0:T(8,128)(2,1)S(1)} %fusion.12, bf16[128,2048]{1,0:T(8,128)(2,1)S(1)} %copy-done.1), kind=kOutput, calls=%fused_computation.8 | convolution fusion | flops 404226048 | bytes 3866624 | tf_op jit(solution)/shard_map/dot_general | solution.py:39
  24.8 36.9 %all-to-all-done.1 = bf16[32,24,2048]{2,1,0:T(8,128)(2,1)} async-done(((bf16[32,24,2048]{2,1,0:T(8,128)(2,1)}), bf16[32,24,2048]{2,1,0:T(8,128)(2,1)}, u32[]{:S(2)}, u32[]{:S(2)}) %all-to-all-start.1) | async-done | bytes 3145760 | tf_op jit(solution)/shard_map/all_to_all | solution.py:55
  61.7 6.8 %all-to-all-start = ((bf16[32,24,2048]{2,1,0:T(8,128)(2,1)}), bf16[32,24,2048]{2,1,0:T(8,128)(2,1)}, u32[]{:S(2)}, u32[]{:S(2)}) async-start(bf16[32,24,2048]{2,1,0:T(8,128)(2,1)} %bitcast.44), calls=%async_computation | async-start | bytes 6291456 | tf_op jit(solution)/shard_map/all_to_all | solution.py:55
  68.5 19.6 %all-gather.2.cloned.1.call-done = bf16[2048,1536]{1,0:T(8,128)(2,1)} async-done(((bf16[256,1536]{1,0:T(8,128)(2,1)}), bf16[2048,1536]{1,0:T(8,128)(2,1)}) %all-gather.2.cloned.1.call-update) | async-done | bytes 6291472 | tf_op jit(solution)/shard_map/all_gather | solution.py:50
  88.1 8.3 %fusion.2 = f32[768,1024]{0,1:T(8,128)} fusion(bf16[768,2048]{1,0:T(8,128)(2,1)} %bitcast.11, bf16[2048,1536]{1,0:T(8,128)(2,1)} %all-gather.2.cloned.1.call-done), kind=kOutput, calls=%fused_computation.4 | convolution fusion | flops 3221225472 | bytes 10485760 | tf_op jit(solution)/shard_map/dot_general | solution.py:39
  96.4 11.9 %all-to-all-done = bf16[32,24,2048]{2,1,0:T(8,128)(2,1)} async-done(((bf16[32,24,2048]{2,1,0:T(8,128)(2,1)}), bf16[32,24,2048]{2,1,0:T(8,128)(2,1)}, u32[]{:S(2)}, u32[]{:S(2)}) %all-to-all-start) | async-done | bytes 3145760 | tf_op jit(solution)/shard_map/all_to_all | solution.py:55
  108.2 4.9 %convolution_convert_fusion.3 = bf16[2048,512]{1,0:T(8,128)(2,1)S(1)} fusion(bf16[768,2048]{1,0:T(8,128)(2,1)} %bitcast.5, f32[768,1024]{0,1:T(8,128)} %fusion.2), kind=kOutput, calls=%fused_computation.9 | convolution fusion | flops 1614020608 | bytes 8388608 | tf_op jit(solution)/shard_map/dot_general | solution.py:39
  113.2 4.9 %multiply_convert_fusion.2 = (bf16[768,512]{0,1:T(8,128)(2,1)S(1)}, bf16[768,512]{0,1:T(8,128)(2,1)S(1)}) fusion(f32[768,1024]{0,1:T(8,128)S(1)} %copy-done.4, bf16[768,2048]{1,0:T(8,128)(2,1)} %bitcast.5, bf16[2048,1536]{1,0:T(8,128)(2,1)} %all-gather.2.cloned.1.call-done), kind=kOutput, calls=%fused_computation.17 | convolution fusion | flops 1615724544 | bytes 9961472 | tf_op jit(solution)/shard_map/dot_general | solution.py:39
  118.1 6.7 %convolution_convert_fusion = bf16[2048,1024]{1,0:T(8,128)(2,1)S(1)} fusion(bf16[768,2048]{1,0:T(8,128)(2,1)} %bitcast.11, bf16[768,512]{0,1:T(8,128)(2,1)S(1)} %get-tuple-element.21, bf16[768,512]{0,1:T(8,128)(2,1)S(1)} %get-tuple-element.20), kind=kOutput, calls=%fused_computation.1 | convolution fusion | flops 3226468352 | bytes 8912896 | tf_op jit(solution)/shard_map/dot_general | solution.py:39
  124.8 3.2 %pad_maximum_fusion = bf16[2048,1536]{1,0:T(8,128)(2,1)} fusion(bf16[2048,512]{1,0:T(8,128)(2,1)S(1)} %convolution_convert_fusion.3, bf16[2048,1024]{1,0:T(8,128)(2,1)S(1)} %convolution_convert_fusion), kind=kLoop, calls=%fused_computation | loop fusion | flops 12582912 | bytes 12582912 | tf_op jit(solution)/shard_map/concatenate | solution.py:81
  128.0 6.0 %fusion.4 = bf16[768,2048]{1,0:T(8,128)(2,1)S(1)} fusion(bf16[2048,1536]{1,0:T(8,128)(2,1)} %all-gather.2.cloned.1.call-done, bf16[768,512]{0,1:T(8,128)(2,1)S(1)} %get-tuple-element.21, bf16[768,512]{0,1:T(8,128)(2,1)S(1)} %get-tuple-element.20), kind=kOutput, calls=%fused_computation.6 | convolution fusion | flops 3225944064 | bytes 8912896 | tf_op jit(solution)/shard_map/dot_general | solution.py:39
  134.0 43.7 %all_to_all.15 = bf16[32,24,2048]{2,1,0:T(8,128)(2,1)S(1)} all-to-all(bf16[32,24,2048]{2,1,0:T(8,128)(2,1)S(1)} %bitcast.45), channel_id=1, replica_groups=mesh['expert'=32,'dp'=8] {'expert'}, dimensions={0} | all-to-all | bytes 6291456 | tf_op jit(solution)/shard_map/all_to_all | solution.py:55
  177.8 1.4 fusion.7
  179.2 24.2 %reduce-scatter.2.cloned.1.call-done = bf16[256,1536]{1,0:T(8,128)(2,1)} async-done(((bf16[2048,1536]{1,0:T(8,128)(2,1)}), bf16[256,1536]{1,0:T(8,128)(2,1)}) %reduce-scatter.2.cloned.1.call-update) | async-done | bytes 786448 | tf_op jit(solution)/shard_map/reduce_scatter | solution.py:82
  203.4 2.0 slice_bitcast_fusion
  205.4 0.8 copy.43
  (18 shorter events, 0.2 us)
Async XLA Ops:
  7.2 4.3 %copy-start = (bf16[128,2048]{1,0:T(8,128)(2,1)S(1)}, bf16[128,2048]{1,0:T(8,128)(2,1)}, u32[]{:S(2)}) copy-start(bf16[128,2048]{1,0:T(8,128)(2,1)} %param.7) | copy-start | bytes 1572868
  7.2 80.9 %all-gather.2.cloned.1.call-start = ((), (), s32[]{:S(2)}) async-start(), calls=%async_computation.4 | async-start | bytes 7077888 | tf_op jit(solution)/shard_map/all_gather | solution.py:50
  14.1 7.8 %copy-start.3 = (bf16[128,4]{0,1:T(4,128)(2,1)S(1)}, bf16[128,4]{0,1:T(4,128)(2,1)}, u32[]{:S(2)}) copy-start(bf16[128,4]{0,1:T(4,128)(2,1)} %param.10) | copy-start | bytes 3076
  14.1 7.8 %copy-start.2 = (s32[128,4]{0,1:T(4,128)S(1)}, s32[128,4]{0,1:T(4,128)}, u32[]{:S(2)}) copy-start(s32[128,4]{0,1:T(4,128)} %param.9) | copy-start | bytes 6148
  14.1 8.0 %copy-start.1 = (bf16[128,2048]{1,0:T(8,128)(2,1)S(1)}, bf16[128,2048]{1,0:T(8,128)(2,1)}, u32[]{:S(2)}) copy-start(bf16[128,2048]{1,0:T(8,128)(2,1)} %param.8) | copy-start | bytes 1572868
  14.1 47.5 %all-to-all-start.1 = ((bf16[32,24,2048]{2,1,0:T(8,128)(2,1)}), bf16[32,24,2048]{2,1,0:T(8,128)(2,1)}, u32[]{:S(2)}, u32[]{:S(2)}) async-start(bf16[32,24,2048]{2,1,0:T(8,128)(2,1)} %bitcast.43), calls=%async_computation.1 | async-start | bytes 6291456 | tf_op jit(solution)/shard_map/all_to_all | solution.py:55
  61.7 46.6 %all-to-all-start = ((bf16[32,24,2048]{2,1,0:T(8,128)(2,1)}), bf16[32,24,2048]{2,1,0:T(8,128)(2,1)}, u32[]{:S(2)}, u32[]{:S(2)}) async-start(bf16[32,24,2048]{2,1,0:T(8,128)(2,1)} %bitcast.44), calls=%async_computation | async-start | bytes 6291456 | tf_op jit(solution)/shard_map/all_to_all | solution.py:55
  68.4 135.0 %reduce-scatter.2.cloned.1.call-start = ((), (), s32[]{:S(2)}) async-start(), calls=%async_computation.5 | async-start | bytes 7077888 | tf_op jit(solution)/shard_map/reduce_scatter | solution.py:82
  108.2 4.9 %copy-start.4 = (f32[768,1024]{0,1:T(8,128)S(1)}, f32[768,1024]{0,1:T(8,128)}, u32[]{:S(2)}) copy-start(f32[768,1024]{0,1:T(8,128)} %fusion.2) | copy-start | bytes 9437188
Sparse Core Ops, SparseCore 0:
  10.5 77.5 all-gather.1
  128.1 75.2 reduce-scatter.1

commit v2 on v1

v2 whole, which is shorter than its diff:
```python
import jax
import jax.numpy as jnp
from jax import lax
from jax.experimental import pallas as pl
from jax.experimental.pallas import tpu as pltpu
from jax.sharding import PartitionSpec as P

ROWS = 256
COLS = 256


def matmul(a, b, dims=((1,), (0,))):
    return lax.dot_general(a, b, (dims, ((), ())), preferred_element_type=jnp.float32)


def pack_kernel(capacity, routes_ref, gate_ref, tokens_ref, cotangent_ref, packed_ref, rank_ref):
    some, tok_dev = rank_ref.shape
    fan_out = routes_ref.shape[0]
    width = tokens_ref.shape[1]
    ids = lax.broadcasted_iota(jnp.int32, (some, tok_dev), 0) + pl.program_id(0) * some
    member = jnp.zeros((some, tok_dev), jnp.float32)
    gate = jnp.zeros((some, tok_dev), jnp.float32)
    for k in range(fan_out):
        hit = routes_ref[k : k + 1, :] == ids
        member = jnp.where(hit, 1.0, member)
        gate = jnp.where(hit, gate_ref[k : k + 1, :], gate)
    row = lax.broadcasted_iota(jnp.int32, (tok_dev, tok_dev), 0)
    col = lax.broadcasted_iota(jnp.int32, (tok_dev, tok_dev), 1)
    before = matmul(member.astype(jnp.bfloat16), (row < col).astype(jnp.bfloat16))
    rank = jnp.where(member > 0.5, before, -1.0)
    rank_ref[...] = rank.astype(jnp.int32)
    slots = lax.broadcasted_iota(jnp.int32, (capacity, tok_dev), 0).astype(jnp.float32)
    place, weighted = [], []
    for e in range(some):
        here = jnp.broadcast_to(rank[e : e + 1, :], (capacity, tok_dev)) == slots
        place.append(jnp.where(here, 1.0, 0.0))
        weighted.append(
            jnp.where(here, jnp.broadcast_to(gate[e : e + 1, :], (capacity, tok_dev)), 0.0)
        )
    place = jnp.concatenate(place, axis=0).astype(jnp.bfloat16)
    weighted = jnp.concatenate(weighted, axis=0).astype(jnp.bfloat16)
    packed_ref[:, :width] = matmul(place, tokens_ref[...]).astype(packed_ref.dtype)
    packed_ref[:, width:] = matmul(weighted, cotangent_ref[...]).astype(packed_ref.dtype)


def pack(routes, gate_values, tokens, cotangent, experts, capacity):
    tok_dev, width = tokens.shape
    fan_out = routes.shape[1]
    some = 8

    def whole(*shape):
        return pl.BlockSpec(shape, lambda i: (0, 0))

    return pl.pallas_call(
        lambda *refs: pack_kernel(capacity, *refs),
        grid=(experts // some,),
        in_specs=[
            whole(fan_out, tok_dev),
            whole(fan_out, tok_dev),
            whole(tok_dev, width),
            whole(tok_dev, width),
        ],
        out_specs=[
            pl.BlockSpec((some * capacity, 2 * width), lambda i: (i, 0)),
            pl.BlockSpec((some, tok_dev), lambda i: (i, 0)),
        ],
        out_shape=[
            jax.ShapeDtypeStruct((experts * capacity, 2 * width), tokens.dtype),
            jax.ShapeDtypeStruct((experts, tok_dev), jnp.int32),
        ],
        compiler_params=pltpu.CompilerParams(vmem_limit_bytes=60 << 20),
        cost_estimate=pl.CostEstimate(
            flops=4 * experts * capacity * tok_dev * width,
            bytes_accessed=4 * experts * capacity * width,
            transcendentals=0,
        ),
        name="pack",
    )(routes.T, gate_values.T.astype(jnp.float32), tokens, cotangent)


def stack_kernel(gate_ref, up_ref, down_ref, rank_ref, out_ref):
    out_ref[0] = gate_ref[0]
    out_ref[1] = up_ref[0]
    out_ref[2] = down_ref[0].T


def stack(w_gate, w_up, w_down, rank):
    _, rows, width = w_gate.shape
    return pl.pallas_call(
        stack_kernel,
        in_specs=[pl.BlockSpec(memory_space=pltpu.VMEM)] * 3 + [pl.BlockSpec(memory_space=pl.ANY)],
        out_specs=pl.BlockSpec(memory_space=pltpu.VMEM),
        out_shape=jax.ShapeDtypeStruct((3, rows, width), w_gate.dtype),
        compiler_params=pltpu.CompilerParams(vmem_limit_bytes=60 << 20),
        name="stack",
    )(w_gate, w_up, w_down, rank)


def terms_kernel(row_steps, rows_ref, x_ref, scaled_ref, w_ref, grads_ref, terms_ref, grads, hidden_t):
    i = pl.program_id(0)
    width = w_ref.shape[1]
    ff = w_ref.shape[2]

    @pl.when(i < row_steps)
    def _():
        x = rows_ref[:, :width]
        gate_pre = matmul(x, w_ref[0])
        up_pre = matmul(x, w_ref[1])
        hidden_grad = matmul(rows_ref[:, width:], w_ref[2])
        sig = 1.0 / (1.0 + jnp.exp(-gate_pre))
        activated = gate_pre * sig
        hidden = activated * up_pre
        gate_grad = hidden_grad * up_pre * sig * (1.0 + gate_pre * (1.0 - sig))
        up_grad = hidden_grad * activated
        start = pl.multiple_of(i * ROWS, ROWS)
        both = jnp.concatenate(
            [gate_grad.astype(jnp.bfloat16), up_grad.astype(jnp.bfloat16)], axis=1
        )
        grads[pl.ds(start, ROWS), :] = both
        grads_ref[...] = both
        hidden_t[:, pl.ds(start, ROWS)] = hidden.astype(jnp.bfloat16).T

    @pl.when(i >= row_steps)
    def _():
        both = matmul(x_ref[...], grads[...], ((0,), (0,))).astype(jnp.bfloat16)
        terms_ref[0] = both[:, :ff]
        terms_ref[1] = both[:, ff:]
        down = matmul(hidden_t[...], scaled_ref[...]).astype(jnp.bfloat16)
        terms_ref[2] = jnp.concatenate([down[: ff // 2], down[ff // 2 :]], axis=1)


def terms_of(received, full):
    rows, width2 = received.shape
    _, width, ff = full.shape
    row_steps, col_steps = rows // ROWS, width // COLS

    def col(i):
        return jnp.maximum(i - row_steps, 0)

    def row(i):
        return jnp.minimum(i, row_steps - 1)

    return pl.pallas_call(
        lambda *refs: terms_kernel(row_steps, *refs),
        grid=(row_steps + col_steps,),
        in_specs=[
            pl.BlockSpec((ROWS, width2), lambda i: (row(i), 0)),
            pl.BlockSpec((rows, COLS), lambda i: (0, col(i))),
            pl.BlockSpec((rows, COLS), lambda i: (0, col_steps + col(i))),
            pl.BlockSpec((3, width, ff), lambda i: (0, 0, 0), pipeline_mode=pl.Buffered(1)),
        ],
        out_specs=[
            pl.BlockSpec((ROWS, 2 * ff), lambda i: (row(i), 0)),
            pl.BlockSpec((3, COLS, ff), lambda i: (0, col(i), 0)),
        ],
        out_shape=[
            jax.ShapeDtypeStruct((rows, 2 * ff), jnp.bfloat16),
            jax.ShapeDtypeStruct((3, width, ff), jnp.bfloat16),
        ],
        scratch_shapes=[
            pltpu.VMEM((rows, 2 * ff), jnp.bfloat16),
            pltpu.VMEM((ff, rows), jnp.bfloat16),
        ],
        compiler_params=pltpu.CompilerParams(vmem_limit_bytes=60 << 20),
        cost_estimate=pl.CostEstimate(
            flops=12 * rows * width * ff,
            bytes_accessed=2 * (4 * rows * width + 6 * width * ff),
            transcendentals=rows * ff,
        ),
        name="terms",
    )(received, received, received, full)


def split_kernel(sums_ref, gate_ref, up_ref, down_ref):
    gate_ref[0] = sums_ref[0]
    up_ref[0] = sums_ref[1]
    half = sums_ref.shape[1]
    down_ref[0, :half] = sums_ref[2, :, : COLS]
    down_ref[0, half:] = sums_ref[2, :, COLS :]


def split(sums):
    _, rows, ff = sums.shape
    vmem = pl.BlockSpec(memory_space=pltpu.VMEM)
    return pl.pallas_call(
        split_kernel,
        in_specs=[vmem],
        out_specs=[vmem] * 3,
        out_shape=[
            jax.ShapeDtypeStruct((1, rows, ff), sums.dtype),
            jax.ShapeDtypeStruct((1, rows, ff), sums.dtype),
            jax.ShapeDtypeStruct((1, ff, rows), sums.dtype),
        ],
        compiler_params=pltpu.CompilerParams(vmem_limit_bytes=60 << 20),
        name="split",
    )(sums)


def local(tokens, cotangent, routes, gate_values, w_gate, w_up, w_down):
    experts = lax.axis_size("expert")
    tok_dev, model_width = tokens.shape
    fan_out = routes.shape[1]
    capacity = min(tok_dev, 3 * tok_dev * fan_out // (2 * experts))

    def exchange(rows):
        return lax.all_to_all(
            rows.reshape(experts, capacity, rows.shape[1]),
            "expert",
            split_axis=0,
            concat_axis=0,
            tiled=True,
        ).reshape(rows.shape)

    packed, rank = pack(routes, gate_values, tokens, cotangent, experts, capacity)
    received = exchange(packed)
    full = lax.all_gather(stack(w_gate, w_up, w_down, rank), "dp", axis=1, tiled=True)

    both_grad, terms = terms_of(received, full)
    sums = lax.psum_scatter(terms, "dp", scatter_dimension=1, tiled=True)

    ff = w_gate.shape[2]
    row_grad = matmul(both_grad[:, :ff], full[0], ((1,), (1,))) + matmul(
        both_grad[:, ff:], full[1], ((1,), (1,))
    )
    returned = exchange(row_grad.astype(jnp.bfloat16))
    place = rank[:, None, :] == jnp.arange(capacity, dtype=jnp.int32)[None, :, None]
    place = place.reshape(experts * capacity, tok_dev).astype(jnp.bfloat16)
    token_grad = matmul(place, returned, ((0,), (0,))).astype(jnp.bfloat16)
    return (token_grad, *split(sums))


def solution(mesh):
    in_specs = (
        P(("expert", "dp"), None),
        P(("expert", "dp"), None),
        P(("expert", "dp"), None),
        P(("expert", "dp"), None),
        P("expert", "dp", None),
        P("expert", "dp", None),
        P("expert", None, "dp"),
    )
    out_specs = (
        P(("expert", "dp"), None),
        P("expert", "dp", None),
        P("expert", "dp", None),
        P("expert", None, "dp"),
    )
    return jax.shard_map(local, mesh=mesh, in_specs=in_specs, out_specs=out_specs, check_vma=False)
```

time: 214 us -> 203 us (0.949)
  blocking collectives: 43.7 us -> 124 us
  waiting for transfers between devices: 92.6 us -> 21.2 us
  Pallas kernels: 0 us -> 29.2 us
  matrix products: 37.6 us -> 9.63 us
  starting transfers between devices: 14.6 us -> 0.08 us
  other arithmetic: 6.23 us -> 1.26 us
  local copies, waits for them, and re-layouts: 4.04 us -> 1.39 us
    all_to_all x1 -> x2, blocking collectives: 43.7 us -> 124 us  [exchange(): lax.all_to_all(rows.reshape(experts, capacity, rows.shape[1]), 'expert',...]
    all_to_all x2 -> x0, waiting for transfers between devices: 48.8 us -> none  [exchange(): lax.all_to_all(rows.reshape(experts, capacity, model_width), 'expert', sp...]
    pallas_call x0 -> x4, Pallas kernels: none -> 29.2 us  [the longest x1 19.4 us: terms_of(): pl.pallas_call(lambda *refs: terms_kernel(row_steps, *refs), grid=(row_st...]
    dot_general x8 -> x3, matrix products: 37.5 us -> 9.63 us  [matmul(): lax.dot_general(a, b, (dims, ((), ())), preferred_element_type=jnp.float32)]
    all_gather x1, waiting for transfers between devices: 19.6 us -> 0.01 us  [local(): lax.all_gather(stack(w_gate, w_up, w_down, rank), 'dp', axis=1, tiled=True)]
    all_to_all x2 -> x0, starting transfers between devices: 14.6 us -> none  [exchange(): lax.all_to_all(rows.reshape(experts, capacity, model_width), 'expert', sp...]
    concatenate x2 -> x0, other arithmetic: 5.17 us -> none  [the longest x1 3.19 us: local(): terms = jnp.concatenate([in_term, down_term], axis=1)]
    reduce_scatter x1, waiting for transfers between devices: 24.2 us -> 21.2 us  [local(): sums = lax.psum_scatter(terms, 'dp', scatter_dimension=1, tiled=True)]
  transfers between devices with their start and end apart: 4 -> 2, of which waited for: 4 -> 1; matrix products, arithmetic and copies ran while one was open for 10% -> 5% of each run, Pallas kernels for 0% -> 0%
where the time goes in v2:
time: 203 us; the launch traced here: 201 us
  blocking collectives  124 us (61%)
  Pallas kernels  29.2 us (14%)
  waiting for transfers between devices  21.2 us (10%)
  between operations  14.1 us (7%)
  matrix products  9.63 us (5%)
    all_to_all x2, blocking collectives, exchange(): lax.all_to_all(rows.reshape(experts, capacity, rows.shape[1]), 'expert',...  124 us
    reduce_scatter x1, waiting for transfers between devices, local(): sums = lax.psum_scatter(terms, 'dp', scatter_dimension=1, tiled=True)  21.2 us
    pallas_call x1, Pallas kernels, terms_of(): pl.pallas_call(lambda *refs: terms_kernel(row_steps, *refs), grid=(row_st...  19.4 us
    dot_general x3, matrix products, matmul(): lax.dot_general(a, b, (dims, ((), ())), preferred_element_type=jnp.float32)  9.63 us
    pallas_call x1, Pallas kernels, pack(): pl.pallas_call(lambda *refs: pack_kernel(capacity, *refs), grid=(experts...  5.66 us
  transfers between devices with their start and end apart: 2, of which 1 were waited for; matrix products, arithmetic and copies ran while one was open for 5% of the time, Pallas kernels for 0%

profile of v2, /device:TPU:2, one launch (start us, length us, event | category | flops | bytes accessed | tf_op | source)
XLA Modules:
  0.0 201.0 jit_solution(13921370384880702124)
XLA Ops:
  7.2 0.0 all-gather.2.cloned.1.call-start
  7.2 1.3 convert_bitcast_fusion.refs_1_
  8.5 5.7 %pack.1 = (bf16[768,4096]{1,0:T(8,128)(2,1)}, s32[32,128]{1,0:T(8,128)}) custom-call(s32[4,128]{1,0:T(4,128)} %bitcast.21, f32[4,128]{1,0:T(4,128)} %convert_bitcast_fusion.refs_1_, bf16[128,2048]{1,0:T(8,128)(2,1)} %refs_2_.1, bf16[128,2048]{1,0:T(8,128)(2,1)} %refs_3_.1), custom_call_target="tpu_custom_call" | custom-call | flops 805306368 | bytes 6291456 | tf_op jit(solution)/shard_map/pack/pallas_call | solution.py:54
  14.1 2.1 %stack.1 = bf16[3,256,512]{2,1,0:T(8,128)(2,1)} custom-call(bf16[1,256,512]{2,1,0:T(8,128)(2,1)} %gate_ref.1, bf16[1,256,512]{2,1,0:T(8,128)(2,1)} %up_ref.1, bf16[1,512,256]{2,1,0:T(8,128)(2,1)} %down_ref.1, s32[32,128]{1,0:T(8,128)} %get-tuple-element.11.rank_ref), custom_call_target="tpu_custom_call" | custom-call | tf_op jit(solution)/shard_map/stack/pallas_call | solution.py:89
  16.2 0.0 all-gather.2.cloned.1.call-update
  16.3 0.0 reduce-scatter.2.cloned.1.call-start
  16.3 80.0 %all_to_all.10 = bf16[32,24,4096]{2,1,0:T(8,128)(2,1)} all-to-all(bf16[32,24,4096]{2,1,0:T(8,128)(2,1)} %bitcast.17), channel_id=1, replica_groups=mesh['expert'=32,'dp'=8] {'expert'}, dimensions={0} | all-to-all | bytes 12582912 | tf_op jit(solution)/shard_map/all_to_all | solution.py:206
  96.3 0.0 all-gather.2.cloned.1.call-done.refs_3_
  96.3 19.4 %terms.1 = (bf16[768,1024]{1,0:T(8,128)(2,1)}, bf16[3,2048,512]{2,1,0:T(8,128)(2,1)}) custom-call(bf16[768,4096]{1,0:T(8,128)(2,1)} %bitcast.18, bf16[768,4096]{1,0:T(8,128)(2,1)} %bitcast.19, bf16[768,4096]{1,0:T(8,128)(2,1)} %bitcast.20, bf16[3,2048,512]{2,1,0:T(8,128)(2,1)} %all-gather.2.cloned.1.call-done.refs_3_), custom_call_target="tpu_custom_call" | custom-call | flops 9663676416 | bytes 25165824 | tf_op jit(solution)/shard_map/terms/pallas_call | solution.py:143
  115.8 0.0 copy-start
  115.8 0.0 reduce-scatter.2.cloned.1.call-update
  115.8 1.4 copy-done
  117.2 3.4 %fusion.8 = f32[768,2048]{1,0:T(8,128)S(1)} fusion(bf16[3,2048,512]{2,1,0:T(8,128)(2,1)} %all-gather.2.cloned.1.call-done.refs_3_, bf16[768,1024]{1,0:T(8,128)(2,1)S(1)} %copy-done), kind=kOutput, calls=%fused_computation.7 | convolution fusion | flops 1610612736 | bytes 9175040 | tf_op jit(solution)/shard_map/dot_general | solution.py:13
  120.6 3.5 %add_convert_fusion = bf16[768,2048]{1,0:T(8,128)(2,1)S(1)} fusion(f32[768,2048]{1,0:T(8,128)S(1)} %fusion.8, bf16[3,2048,512]{2,1,0:T(8,128)(2,1)} %all-gather.2.cloned.1.call-done.refs_3_, bf16[768,1024]{1,0:T(8,128)(2,1)S(1)} %copy-done), kind=kOutput, calls=%fused_computation | convolution fusion | flops 1613758464 | bytes 12320768 | tf_op jit(solution)/shard_map/dot_general | solution.py:13
  124.0 0.0 copy-start.1
  124.0 44.1 %all_to_all.11 = bf16[32,24,2048]{2,1,0:T(8,128)(2,1)S(1)} all-to-all(bf16[32,24,2048]{2,1,0:T(8,128)(2,1)S(1)} %bitcast.16), channel_id=1, replica_groups=mesh['expert'=32,'dp'=8] {'expert'}, dimensions={0} | all-to-all | bytes 6291456 | tf_op jit(solution)/shard_map/all_to_all | solution.py:206
  168.2 0.0 copy-done.1
  168.2 2.8 %fusion.5 = bf16[128,2048]{1,0:T(8,128)(2,1)} fusion(bf16[32,24,2048]{2,1,0:T(8,128)(2,1)S(1)} %all_to_all.11, s32[32,128]{1,0:T(8,128)S(1)} %copy-done.1), kind=kOutput, calls=%fused_computation.4 | convolution fusion | flops 403013632 | bytes 3686400 | tf_op jit(solution)/shard_map/dot_general | solution.py:13
  171.0 21.2 %reduce-scatter.2.cloned.1.call-done.sums_ref = bf16[3,256,512]{2,1,0:T(8,128)(2,1)} async-done(((bf16[3,2048,512]{2,1,0:T(8,128)(2,1)}), bf16[3,256,512]{2,1,0:T(8,128)(2,1)}) %reduce-scatter.2.cloned.1.call-update) | async-done | bytes 786448 | tf_op jit(solution)/shard_map/reduce_scatter | solution.py:219
  192.1 2.0 %split.1 = (bf16[1,256,512]{2,1,0:T(8,128)(2,1)}, bf16[1,256,512]{2,1,0:T(8,128)(2,1)}, bf16[1,512,256]{2,1,0:T(8,128)(2,1)}) custom-call(bf16[3,256,512]{2,1,0:T(8,128)(2,1)} %reduce-scatter.2.cloned.1.call-done.sums_ref), custom_call_target="tpu_custom_call" | custom-call | tf_op jit(solution)/shard_map/split/pallas_call | solution.py:185
Async XLA Ops:
  7.2 89.2 %all-gather.2.cloned.1.call-start = ((), (), s32[]{:S(2)}) async-start(), calls=%async_computation.3 | async-start | bytes 7077888 | tf_op jit(solution)/shard_map/all_gather | solution.py:216
  16.3 175.8 %reduce-scatter.2.cloned.1.call-start = ((), (), s32[]{:S(2)}) async-start(), calls=%async_computation.4 | async-start | bytes 7077888 | tf_op jit(solution)/shard_map/reduce_scatter | solution.py:219
  115.8 1.4 copy-start
  124.0 44.2 %copy-start.1 = (s32[32,128]{1,0:T(8,128)S(1)}, s32[32,128]{1,0:T(8,128)}, u32[]{:S(2)}) copy-start(s32[32,128]{1,0:T(8,128)} %get-tuple-element.11.rank_ref) | copy-start | bytes 49156
Sparse Core Ops, SparseCore 0:
  16.4 77.4 all-gather.1
  115.9 76.1 reduce-scatter.1

commit v3 on v2

v3 whole, which is shorter than its diff:
```python
import jax
import jax.numpy as jnp
from jax import lax
from jax.experimental import pallas as pl
from jax.experimental.pallas import tpu as pltpu
from jax.sharding import PartitionSpec as P

ROWS = 384
COLS = 256
TERM_COLS = 512
PACK_COLS = 512


def matmul(a, b, dims=((1,), (0,))):
    return lax.dot_general(a, b, (dims, ((), ())), preferred_element_type=jnp.float32)


def pack_kernel(
    capacity,
    routes_ref,
    gate_ref,
    tokens_hbm,
    cotangent_hbm,
    w_gate_hbm,
    w_up_hbm,
    w_down_hbm,
    packed_hbm,
    rank_ref,
    shard_hbm,
    tokens,
    shards,
    down,
    place,
    packed,
    in_sems,
    w_sems,
    shard_sems,
    out_sems,
):
    experts, tok_dev = rank_ref.shape
    width = tokens_hbm.shape[1]
    sources = [tokens_hbm, cotangent_hbm]
    row_copies = [
        pltpu.make_async_copy(sources[k], tokens.at[k], in_sems.at[k]) for k in range(2)
    ]
    w_copies = [
        pltpu.make_async_copy(w_gate_hbm.at[0], shards.at[0], w_sems.at[0]),
        pltpu.make_async_copy(w_up_hbm.at[0], shards.at[1], w_sems.at[1]),
        pltpu.make_async_copy(w_down_hbm.at[0], down, w_sems.at[2]),
    ]
    for copy in row_copies + w_copies:
        copy.start()

    ids = lax.broadcasted_iota(jnp.int32, (experts, tok_dev), 0)
    gates = gate_ref[...].astype(jnp.float32)
    member = jnp.zeros((experts, tok_dev), jnp.float32)
    gate = jnp.zeros((experts, tok_dev), jnp.float32)
    for k in range(routes_ref.shape[0]):
        hit = routes_ref[k : k + 1, :] == ids
        member = jnp.where(hit, 1.0, member)
        gate = jnp.where(hit, gates[k : k + 1, :], gate)
    row = lax.broadcasted_iota(jnp.int32, (tok_dev, tok_dev), 0)
    col = lax.broadcasted_iota(jnp.int32, (tok_dev, tok_dev), 1)
    before = matmul(member.astype(jnp.bfloat16), (row < col).astype(jnp.bfloat16))
    rank = jnp.where(member > 0.5, before, -1.0)
    rank_ref[...] = rank.astype(jnp.int32)
    slots = lax.broadcasted_iota(jnp.int32, (capacity, tok_dev), 0).astype(jnp.float32)
    for e in range(0, experts, 2):
        here, gate_here = [], []
        for f in (e, e + 1):
            mask = jnp.broadcast_to(rank[f : f + 1, :], (capacity, tok_dev)) == slots
            here.append(jnp.where(mask, 1.0, 0.0))
            gate_here.append(
                jnp.where(mask, jnp.broadcast_to(gate[f : f + 1, :], (capacity, tok_dev)), 0.0)
            )
        span = slice(e * capacity, (e + 2) * capacity)
        place[0, span, :] = jnp.concatenate(here, axis=0).astype(place.dtype)
        place[1, span, :] = jnp.concatenate(gate_here, axis=0).astype(place.dtype)

    shard_copies = [
        pltpu.make_async_copy(shards.at[k], shard_hbm.at[k], shard_sems.at[k]) for k in range(3)
    ]
    out_copies = []
    for k in range(2):
        row_copies[k].wait()
        for start in range(0, width, PACK_COLS):
            span = slice(k * width + start, k * width + start + PACK_COLS)
            packed[:, span] = matmul(
                place[k], tokens[k, :, start : start + PACK_COLS]
            ).astype(packed.dtype)
            cols = (slice(None), pl.ds(k * width + start, PACK_COLS))
            out_copies.append(
                pltpu.make_async_copy(
                    packed.at[cols], packed_hbm.at[cols], out_sems.at[len(out_copies)]
                )
            )
            out_copies[-1].start()
        if k == 0:
            w_copies[0].wait()
            shard_copies[0].start()
            w_copies[1].wait()
            shard_copies[1].start()
            w_copies[2].wait()
            shards[2] = down[...].T
            shard_copies[2].start()
    for copy in shard_copies + out_copies:
        copy.wait()


def pack(routes, gate_values, tokens, cotangent, w_gate, w_up, w_down, experts, capacity):
    tok_dev, width = tokens.shape
    slots = experts * capacity
    vmem = pl.BlockSpec(memory_space=pltpu.VMEM)
    hbm = pl.BlockSpec(memory_space=pl.ANY)
    return pl.pallas_call(
        lambda *refs: pack_kernel(capacity, *refs),
        in_specs=[vmem] * 2 + [hbm] * 5,
        out_specs=[hbm, vmem, hbm],
        out_shape=[
            jax.ShapeDtypeStruct((slots, 2 * width), tokens.dtype),
            jax.ShapeDtypeStruct((experts, tok_dev), jnp.int32),
            jax.ShapeDtypeStruct((3, *w_gate.shape[1:]), w_gate.dtype),
        ],
        scratch_shapes=[
            pltpu.VMEM((2, tok_dev, width), tokens.dtype),
            pltpu.VMEM((3, *w_gate.shape[1:]), w_gate.dtype),
            pltpu.VMEM(w_down.shape[1:], w_down.dtype),
            pltpu.VMEM((2, slots, tok_dev), jnp.bfloat16),
            pltpu.VMEM((slots, 2 * width), tokens.dtype),
            pltpu.SemaphoreType.DMA((2,)),
            pltpu.SemaphoreType.DMA((3,)),
            pltpu.SemaphoreType.DMA((3,)),
            pltpu.SemaphoreType.DMA((2 * width // PACK_COLS,)),
        ],
        compiler_params=pltpu.CompilerParams(vmem_limit_bytes=60 << 20),
        cost_estimate=pl.CostEstimate(
            flops=4 * slots * tok_dev * width,
            bytes_accessed=4 * slots * width,
            transcendentals=0,
        ),
        name="pack",
    )(routes.T, gate_values.T, tokens, cotangent, w_gate, w_up, w_down)


def terms_kernel(
    rows_hbm,
    w_hbm,
    grads_hbm,
    terms_hbm,
    rows,
    w,
    grads,
    hidden_t,
    terms,
    row_sems,
    w_sems,
    grads_sem,
    out_sems,
):
    _, width, ff = w_hbm.shape
    n = rows.shape[0]

    def row_copy(k, left, size):
        span = (pl.ds(k * ROWS, ROWS), pl.ds(left, size))
        return pltpu.make_async_copy(
            rows_hbm.at[span], rows.at[span], row_sems.at[k + (1 if left else 0) + (k > 0)]
        )

    x_copy = row_copy(0, 0, width)
    scaled_copy = row_copy(0, width, width)
    later = [row_copy(k, 0, 2 * width) for k in range(1, n // ROWS)]
    w_copies = [pltpu.make_async_copy(w_hbm.at[k], w.at[k], w_sems.at[k]) for k in range(3)]
    for copy in [x_copy, *w_copies[:2], scaled_copy, w_copies[2], *later]:
        copy.start()

    for k in range(n // ROWS):
        span = slice(k * ROWS, (k + 1) * ROWS)
        if k == 0:
            x_copy.wait()
            w_copies[0].wait()
        else:
            later[k - 1].wait()
        x = rows[span, :width]
        gate_pre = matmul(x, w[0])
        sig = 1.0 / (1.0 + jnp.exp(-gate_pre))
        activated = gate_pre * sig
        slope = sig * (1.0 + gate_pre * (1.0 - sig))
        if k == 0:
            w_copies[1].wait()
        up_pre = matmul(x, w[1])
        hidden_t[:, span] = (activated * up_pre).astype(jnp.bfloat16).T
        if k == 0:
            scaled_copy.wait()
            w_copies[2].wait()
        hidden_grad = matmul(rows[span, width:], w[2])
        grads[span, :ff] = (hidden_grad * up_pre * slope).astype(jnp.bfloat16)
        grads[span, ff:] = (hidden_grad * activated).astype(jnp.bfloat16)

    out_copies = [pltpu.make_async_copy(grads, grads_hbm, grads_sem)]
    out_copies[0].start()
    for k, start in enumerate(range(0, width, TERM_COLS)):
        span = slice(start, start + TERM_COLS)
        both = matmul(rows[:, span], grads[...], ((0,), (0,))).astype(jnp.bfloat16)
        terms[0, span, :] = both[:, :ff]
        terms[1, span, :] = both[:, ff:]
        down = matmul(hidden_t[...], rows[:, width + start : width + start + TERM_COLS])
        down = down.astype(jnp.bfloat16)
        for c in range(0, TERM_COLS, COLS):
            for h in range(0, ff, COLS):
                terms[2, start + c : start + c + COLS, h : h + COLS] = down[
                    h : h + COLS, c : c + COLS
                ]
        block = (slice(None), pl.ds(start, TERM_COLS), slice(None))
        out_copies.append(
            pltpu.make_async_copy(terms.at[block], terms_hbm.at[block], out_sems.at[k])
        )
        out_copies[-1].start()
    for copy in out_copies:
        copy.wait()


def terms_of(received, full):
    rows, width2 = received.shape
    _, width, ff = full.shape
    hbm = pl.BlockSpec(memory_space=pl.ANY)
    return pl.pallas_call(
        terms_kernel,
        in_specs=[hbm] * 2,
        out_specs=[hbm] * 2,
        out_shape=[
            jax.ShapeDtypeStruct((rows, 2 * ff), jnp.bfloat16),
            jax.ShapeDtypeStruct((3, width, ff), jnp.bfloat16),
        ],
        scratch_shapes=[
            pltpu.VMEM((rows, width2), jnp.bfloat16),
            pltpu.VMEM((3, width, ff), jnp.bfloat16),
            pltpu.VMEM((rows, 2 * ff), jnp.bfloat16),
            pltpu.VMEM((ff, rows), jnp.bfloat16),
            pltpu.VMEM((3, width, ff), jnp.bfloat16),
            pltpu.SemaphoreType.DMA((1 + rows // ROWS,)),
            pltpu.SemaphoreType.DMA((3,)),
            pltpu.SemaphoreType.DMA,
            pltpu.SemaphoreType.DMA((width // TERM_COLS,)),
        ],
        compiler_params=pltpu.CompilerParams(vmem_limit_bytes=60 << 20),
        cost_estimate=pl.CostEstimate(
            flops=12 * rows * width * ff,
            bytes_accessed=2 * (2 * rows * width + 6 * width * ff),
            transcendentals=rows * ff,
        ),
        name="terms",
    )(received, full)


def split_kernel(sums_ref, gate_ref, up_ref, down_ref, held, in_sems, out_sems):
    half = held.shape[1]
    arrive = [pltpu.make_async_copy(sums_ref.at[k], held.at[k], in_sems.at[k]) for k in range(3)]
    leave = [
        [pltpu.make_async_copy(held.at[0], gate_ref.at[0], out_sems.at[0])],
        [pltpu.make_async_copy(held.at[1], up_ref.at[0], out_sems.at[1])],
        [
            pltpu.make_async_copy(
                held.at[2, :, pl.ds(h * half, half)],
                down_ref.at[0, pl.ds(h * half, half), :],
                out_sems.at[2 + h],
            )
            for h in range(2)
        ],
    ]
    for copy in arrive:
        copy.start()
    for copy, copies in zip(arrive, leave):
        copy.wait()
        for c in copies:
            c.start()
    for copies in leave:
        for c in copies:
            c.wait()


def split(sums):
    _, rows, ff = sums.shape
    hbm = pl.BlockSpec(memory_space=pl.ANY)
    return pl.pallas_call(
        split_kernel,
        in_specs=[hbm],
        out_specs=[hbm] * 3,
        out_shape=[
            jax.ShapeDtypeStruct((1, rows, ff), sums.dtype),
            jax.ShapeDtypeStruct((1, rows, ff), sums.dtype),
            jax.ShapeDtypeStruct((1, ff, rows), sums.dtype),
        ],
        scratch_shapes=[
            pltpu.VMEM(sums.shape, sums.dtype),
            pltpu.SemaphoreType.DMA((3,)),
            pltpu.SemaphoreType.DMA((4,)),
        ],
        compiler_params=pltpu.CompilerParams(vmem_limit_bytes=60 << 20),
        name="split",
    )(sums)


def local(tokens, cotangent, routes, gate_values, w_gate, w_up, w_down):
    experts = lax.axis_size("expert")
    tok_dev, model_width = tokens.shape
    fan_out = routes.shape[1]
    capacity = min(tok_dev, 3 * tok_dev * fan_out // (2 * experts))

    def exchange(rows):
        return lax.all_to_all(
            rows.reshape(experts, capacity, rows.shape[1]),
            "expert",
            split_axis=0,
            concat_axis=0,
            tiled=True,
        ).reshape(rows.shape)

    packed, rank, shard = pack(
        routes, gate_values, tokens, cotangent, w_gate, w_up, w_down, experts, capacity
    )
    received = exchange(packed)
    full = lax.all_gather(shard, "dp", axis=1, tiled=True)

    both_grad, terms = terms_of(received, full)
    sums = lax.psum_scatter(terms, "dp", scatter_dimension=1, tiled=True)

    ff = w_gate.shape[2]
    row_grad = matmul(both_grad[:, :ff], full[0], ((1,), (1,))) + matmul(
        both_grad[:, ff:], full[1], ((1,), (1,))
    )
    returned = exchange(row_grad.astype(jnp.bfloat16))
    place = rank[:, None, :] == jnp.arange(capacity, dtype=jnp.int32)[None, :, None]
    place = place.reshape(experts * capacity, tok_dev).astype(jnp.bfloat16)
    token_grad = matmul(place, returned, ((0,), (0,))).astype(jnp.bfloat16)
    return (token_grad, *split(sums))


def solution(mesh):
    in_specs = (
        P(("expert", "dp"), None),
        P(("expert", "dp"), None),
        P(("expert", "dp"), None),
        P(("expert", "dp"), None),
        P("expert", "dp", None),
        P("expert", "dp", None),
        P("expert", None, "dp"),
    )
    out_specs = (
        P(("expert", "dp"), None),
        P("expert", "dp", None),
        P("expert", "dp", None),
        P("expert", None, "dp"),
    )
    return jax.shard_map(local, mesh=mesh, in_specs=in_specs, out_specs=out_specs, check_vma=False)
```

time: 203 us -> 194 us (0.956)
  Pallas kernels: 29.2 us -> 21.8 us
    pallas_call x4 -> x3, Pallas kernels: 29.2 us -> 21.8 us  [the longest x1 14.1 us: terms_of(): pl.pallas_call(terms_kernel, in_specs=[hbm] * 2, out_specs=[hbm] * 2, out...]
where the time goes in v3:
time: 194 us; the launch traced here: 192 us
  blocking collectives  124 us (64%)
  Pallas kernels  21.8 us (11%)
  waiting for transfers between devices  21.2 us (11%)
  between operations  14.1 us (7%)
  matrix products  9.63 us (5%)
    all_to_all x2, blocking collectives, exchange(): lax.all_to_all(rows.reshape(experts, capacity, rows.shape[1]), 'expert',...  124 us
    reduce_scatter x1, waiting for transfers between devices, local(): sums = lax.psum_scatter(terms, 'dp', scatter_dimension=1, tiled=True)  21.2 us
    pallas_call x1, Pallas kernels, terms_of(): pl.pallas_call(terms_kernel, in_specs=[hbm] * 2, out_specs=[hbm] * 2, out...  14.1 us
    dot_general x3, matrix products, matmul(): lax.dot_general(a, b, (dims, ((), ())), preferred_element_type=jnp.float32)  9.63 us
    pallas_call x1, Pallas kernels, pack(): pl.pallas_call(lambda *refs: pack_kernel(capacity, *refs), in_specs=[vmem...  5.83 us
  transfers between devices with their start and end apart: 2, of which 1 were waited for; matrix products, arithmetic and copies ran while one was open for 5% of the time, Pallas kernels for 0%

profile of v3, /device:TPU:2, one launch (start us, length us, event | category | flops | bytes accessed | tf_op | source)
XLA Modules:
  0.0 192.4 jit_solution(13331773423463203858)
XLA Ops:
  7.2 0.0 all-gather.2.cloned.1.call-start
  7.2 5.8 %pack.1 = (bf16[768,4096]{1,0:T(8,128)(2,1)}, s32[32,128]{1,0:T(8,128)}, bf16[3,256,512]{2,1,0:T(8,128)(2,1)}) custom-call(s32[4,128]{1,0:T(4,128)} %bitcast.18, bf16[4,128]{1,0:T(4,128)(2,1)} %bitcast.19, bf16[128,2048]{1,0:T(8,128)(2,1)} %refs_2_.1, bf16[128,2048]{1,0:T(8,128)(2,1)} %refs_3_.1, bf16[1,256,512]{2,1,0:T(8,128)(2,1)} %refs_4_.1, ...), custom_call_target="tpu_custom_call" | custom-call | flops 805306368 | bytes 6291456 | tf_op jit(solution)/shard_map/pack/pallas_call | solution.py:115
  13.0 0.0 all-gather.2.cloned.1.call-update
  13.1 0.0 reduce-scatter.2.cloned.1.call-start
  13.1 80.0 %all_to_all.10 = bf16[32,24,4096]{2,1,0:T(8,128)(2,1)} all-to-all(bf16[32,24,4096]{2,1,0:T(8,128)(2,1)} %bitcast.16), channel_id=1, replica_groups=mesh['expert'=32,'dp'=8] {'expert'}, dimensions={0} | all-to-all | bytes 12582912 | tf_op jit(solution)/shard_map/all_to_all | solution.py:310
  93.1 0.0 all-gather.2.cloned.1.call-done.w_hbm
  93.2 14.1 %terms.1 = (bf16[768,1024]{1,0:T(8,128)(2,1)}, bf16[3,2048,512]{2,1,0:T(8,128)(2,1)}) custom-call(bf16[768,4096]{1,0:T(8,128)(2,1)} %bitcast.17, bf16[3,2048,512]{2,1,0:T(8,128)(2,1)} %all-gather.2.cloned.1.call-done.w_hbm), custom_call_target="tpu_custom_call" | custom-call | flops 9663676416 | bytes 18874368 | tf_op jit(solution)/shard_map/terms/pallas_call | solution.py:226
  107.3 0.0 copy-start
  107.3 0.0 reduce-scatter.2.cloned.1.call-update
  107.3 1.4 copy-done
  108.7 3.4 %fusion.8 = f32[768,2048]{1,0:T(8,128)S(1)} fusion(bf16[3,2048,512]{2,1,0:T(8,128)(2,1)} %all-gather.2.cloned.1.call-done.w_hbm, bf16[768,1024]{1,0:T(8,128)(2,1)S(1)} %copy-done), kind=kOutput, calls=%fused_computation.7 | convolution fusion | flops 1610612736 | bytes 9175040 | tf_op jit(solution)/shard_map/dot_general | solution.py:15
  112.1 3.5 %add_convert_fusion = bf16[768,2048]{1,0:T(8,128)(2,1)S(1)} fusion(f32[768,2048]{1,0:T(8,128)S(1)} %fusion.8, bf16[3,2048,512]{2,1,0:T(8,128)(2,1)} %all-gather.2.cloned.1.call-done.w_hbm, bf16[768,1024]{1,0:T(8,128)(2,1)S(1)} %copy-done), kind=kOutput, calls=%fused_computation | convolution fusion | flops 1613758464 | bytes 12320768 | tf_op jit(solution)/shard_map/dot_general | solution.py:15
  115.6 0.0 copy-start.1
  115.6 44.2 %all_to_all.11 = bf16[32,24,2048]{2,1,0:T(8,128)(2,1)S(1)} all-to-all(bf16[32,24,2048]{2,1,0:T(8,128)(2,1)S(1)} %bitcast.15), channel_id=1, replica_groups=mesh['expert'=32,'dp'=8] {'expert'}, dimensions={0} | all-to-all | bytes 6291456 | tf_op jit(solution)/shard_map/all_to_all | solution.py:310
  159.8 0.0 copy-done.1
  159.8 2.8 %fusion.5 = bf16[128,2048]{1,0:T(8,128)(2,1)} fusion(bf16[32,24,2048]{2,1,0:T(8,128)(2,1)S(1)} %all_to_all.11, s32[32,128]{1,0:T(8,128)S(1)} %copy-done.1), kind=kOutput, calls=%fused_computation.4 | convolution fusion | flops 403013632 | bytes 3686400 | tf_op jit(solution)/shard_map/dot_general | solution.py:15
  162.5 21.2 %reduce-scatter.2.cloned.1.call-done.sums_ref = bf16[3,256,512]{2,1,0:T(8,128)(2,1)} async-done(((bf16[3,2048,512]{2,1,0:T(8,128)(2,1)}), bf16[3,256,512]{2,1,0:T(8,128)(2,1)}) %reduce-scatter.2.cloned.1.call-update) | async-done | bytes 786448 | tf_op jit(solution)/shard_map/reduce_scatter | solution.py:325
  183.7 1.9 split.1
Async XLA Ops:
  7.2 86.0 %all-gather.2.cloned.1.call-start = ((), (), s32[]{:S(2)}) async-start(), calls=%async_computation.3 | async-start | bytes 7077888 | tf_op jit(solution)/shard_map/all_gather | solution.py:322
  13.1 170.6 %reduce-scatter.2.cloned.1.call-start = ((), (), s32[]{:S(2)}) async-start(), calls=%async_computation.4 | async-start | bytes 7077888 | tf_op jit(solution)/shard_map/reduce_scatter | solution.py:325
  107.3 1.4 copy-start
  115.6 44.2 %copy-start.1 = (s32[32,128]{1,0:T(8,128)S(1)}, s32[32,128]{1,0:T(8,128)}, u32[]{:S(2)}) copy-start(s32[32,128]{1,0:T(8,128)} %get-tuple-element.12) | copy-start | bytes 49156
Sparse Core Ops, SparseCore 0:
  13.2 77.4 all-gather.1
  107.4 76.2 reduce-scatter.1
